TPU v7x, 32 devices: a whole 2x2x4 slice. The times are simulated.
32 devices in a mesh: row: 16 (over z, y, core), col: 2 (over x).
Axes of the slice: x: 2, y: 2, z: 4, core: 2. Of those that a mesh axis runs over, the one named last changes fastest.
Arguments:
- layer_input: bfloat16 [16384, 1152], P(('row', 'col')), may hold values from -6 to 6
- attn_gain: bfloat16 [1152], replicated, may hold values from 0.099609375 to 1.8984375
- mlp_gain: bfloat16 [1152], replicated, may hold values from 0.099609375 to 1.8984375
- query_weight: bfloat16 [1152, 1152], P('row', 'col'), may hold values from -0.1875 to 0.1875
- key_weight: bfloat16 [1152, 384], P('row', 'col'), may hold values from -0.1875 to 0.1875
- value_weight: bfloat16 [1152, 384], P('row', 'col'), may hold values from -0.1875 to 0.1875
- out_weight: bfloat16 [1152, 1152], P('col', 'row'), may hold values from -4 to 4
- gate_weight: bfloat16 [1152, 3072], P('row', 'col'), may hold values from -0.1875 to 0.1875
- up_weight: bfloat16 [1152, 3072], P('row', 'col'), may hold values from -0.1875 to 0.1875
- down_weight: bfloat16 [3072, 1152], P('col', 'row'), may hold values from -0.109375 to 0.109375
- seq_ids: int32 [16384], P('row'), may hold values from 0 to 31, as said below
- block_ends: int32 [16384], P('row'), may hold values from 255 to 16383, as said below
- grad_output: bfloat16 [16384, 1152], P(('row', 'col')), may hold values from -6 to 6
Outputs:
- layer_output: bfloat16 [16384, 1152], P(('row', 'col'))
- grad_input: bfloat16 [16384, 1152], P(('row', 'col'))
- grad_attn_gain: float32 [1152], replicated
- grad_mlp_gain: float32 [1152], replicated
- grad_query: float32 [1152, 1152], P('row', 'col')
- grad_key: float32 [1152, 384], P('row', 'col')
- grad_value: float32 [1152, 384], P('row', 'col')
- grad_out_weight: float32 [1152, 1152], P('col', 'row')
- grad_gate: float32 [1152, 3072], P('row', 'col')
- grad_up: float32 [1152, 3072], P('row', 'col')
- grad_down: float32 [3072, 1152], P('col', 'row')
Inputs may be any that keep to these rules, and one draw needn't show every extreme that they name: `seq_ids`: ids never fall; span number s of the aligned spans of 1024 tokens holds exactly two sequences, with ids 2 * s and 2 * s + 1, each of 256 tokens or more. `block_ends`: values never fall; an attention block is a run of 1 to 256 tokens inside one sequence, and the first block of every sequence has exactly 256 tokens.
All inputs are finite; a program needn't handle non-finite values.
Results may differ from a plain program's by a relative error of at most 0.014.
The roundings to bfloat16 on the way count: a program that leaves them out, or rounds other values in their place, can miss the bound.
Values may be sent and summed in bfloat16 or wider, within the bound.
A program may use at most 192 MiB of HBM per device.

v0:
```python
import math
import jax
import jax.numpy as jnp
from jax import lax
from jax.sharding import PartitionSpec as P

QUERY_HEADS = 18
KEY_VALUE_HEADS = 6
HEAD_SIZE_DIM = 64
eps = 1e-05
rope_base = 10000.0
neg_fill = -1e30


def rotate_half(values, head_size):
    lane_index = jnp.arange(values.shape[-1], dtype=jnp.int32) % head_size
    forward_roll = jnp.roll(values, -(head_size // 2), axis=-1)
    backward_roll = jnp.roll(values, head_size // 2, axis=-1)
    return jnp.where(lane_index < head_size // 2, -forward_roll, backward_roll)


def rope_tables(position, table_width, head_size):
    lane_index = (jnp.arange(table_width, dtype=jnp.int32) % (head_size // 2)).astype(jnp.float32)
    frequency = jnp.exp(lane_index * (-2.0 * math.log(rope_base) / head_size))
    angles = position[:, None] * frequency[None, :]
    return (jnp.cos(angles), jnp.sin(angles))


def rotary(values, cosine, sine_part, head_size):
    return values * cosine + rotate_half(values, head_size) * sine_part


def rotary_back(upstream, cosine, sine_part, head_size):
    return upstream * cosine - rotate_half(upstream * sine_part, head_size)


def positions(seq_ids):
    token_index = jnp.arange(seq_ids.shape[0], dtype=jnp.int32)
    earlier = jnp.concatenate([seq_ids[:1] - 1, seq_ids[:-1]])
    seq_start = lax.cummax(jnp.where(seq_ids != earlier, token_index, 0), axis=0)
    return (token_index - seq_start).astype(jnp.float32)


def visible(query_seq, query_end, seq_ids, block_ends):
    return (query_seq[:, None] == seq_ids[None, :]) & (block_ends[None, :] <= query_end[:, None])


def to_rows(values):
    return lax.all_to_all(values, "col", split_axis=0, concat_axis=1, tiled=True)


def to_tokens(values):
    return lax.all_to_all(values, "col", split_axis=1, concat_axis=0, tiled=True)


def col_sums(values):
    return lax.psum_scatter(values, "col", scatter_dimension=0, tiled=True)


def widen(values):
    return lax.all_gather(values, "col", axis=0, tiled=True)


def shards(
    layer_input,
    attn_gain,
    mlp_gain,
    query_weight,
    key_weight,
    value_weight,
    out_weight,
    gate_weight,
    up_weight,
    down_weight,
    seq_ids,
    block_ends,
    grad_output,
):
    col_index = lax.axis_index("col")
    query_rows = layer_input.shape[0]
    block_rows = min(512, query_rows)
    block_count = query_rows // block_rows
    heads_per_group = QUERY_HEADS // KEY_VALUE_HEADS
    group_head_width = heads_per_group * HEAD_SIZE_DIM
    query_width = QUERY_HEADS * HEAD_SIZE_DIM
    score_scale = HEAD_SIZE_DIM ** (-0.5)
    attn_gain_float = attn_gain.astype(jnp.float32)
    mlp_gain_float = mlp_gain.astype(jnp.float32)
    full_input = lax.all_gather(layer_input, "col", axis=0, tiled=True)
    token_rows = full_input.shape[0]
    query_cols, key_cols, value_cols, out_rows, gate_cols, up_cols, down_rows = (
        lax.all_gather(query_weight, "row", axis=0, tiled=True),
        lax.all_gather(key_weight, "row", axis=0, tiled=True),
        lax.all_gather(value_weight, "row", axis=0, tiled=True),
        lax.all_gather(out_weight, "row", axis=1, tiled=True),
        lax.all_gather(gate_weight, "row", axis=0, tiled=True),
        lax.all_gather(up_weight, "row", axis=0, tiled=True),
        lax.all_gather(down_weight, "row", axis=1, tiled=True),
    )
    input_float = full_input.astype(jnp.float32)
    inv_all = lax.rsqrt(jnp.mean(input_float * input_float, axis=1, keepdims=True) + eps)
    attn_in = (input_float * inv_all * attn_gain_float).astype(jnp.bfloat16)
    query_unrotated = jnp.dot(attn_in, query_cols, preferred_element_type=jnp.float32).astype(
        jnp.bfloat16
    )
    key_raw = jnp.dot(attn_in, key_cols, preferred_element_type=jnp.float32).astype(jnp.bfloat16)
    value_projected = jnp.dot(attn_in, value_cols, preferred_element_type=jnp.float32).astype(
        jnp.bfloat16
    )
    query_all = to_rows(query_unrotated)
    key_all, value_all = (
        lax.all_gather(key_raw, "col", axis=1, tiled=True),
        lax.all_gather(value_projected, "col", axis=1, tiled=True),
    )
    position = positions(seq_ids)
    row_start = col_index * query_rows
    query_pos = lax.dynamic_slice_in_dim(position, row_start, query_rows)
    query_seq = lax.dynamic_slice_in_dim(seq_ids, row_start, query_rows)
    query_end = lax.dynamic_slice_in_dim(block_ends, row_start, query_rows)
    query_cos, query_sin = rope_tables(query_pos, query_width, HEAD_SIZE_DIM)
    key_cos, key_sin = rope_tables(position, key_all.shape[1], HEAD_SIZE_DIM)
    query_rotated = (
        rotary(query_all.astype(jnp.float32), query_cos, query_sin, HEAD_SIZE_DIM) * score_scale
    ).astype(jnp.bfloat16)
    key_rotated = rotary(key_all.astype(jnp.float32), key_cos, key_sin, HEAD_SIZE_DIM).astype(
        jnp.bfloat16
    )

    def block_inputs(block_index):
        first_row = block_index * block_rows
        allowed = visible(query_seq, query_end, seq_ids, block_ends)
        return (first_row, allowed)

    def group_scores(query_block, group_index, allowed):
        query_head_rows = lax.dynamic_slice_in_dim(
            query_block, group_index * group_head_width, group_head_width, 1
        ).reshape(block_rows, heads_per_group, HEAD_SIZE_DIM)
        key_group = lax.dynamic_slice_in_dim(
            key_rotated, group_index * HEAD_SIZE_DIM, HEAD_SIZE_DIM, 1
        )
        value_group = lax.dynamic_slice_in_dim(
            value_all, group_index * HEAD_SIZE_DIM, HEAD_SIZE_DIM, 1
        )
        scores = jnp.einsum(
            "qhd,kd->hqk", query_head_rows, key_group, preferred_element_type=jnp.float32
        )
        return (query_head_rows, key_group, value_group, jnp.where(allowed[None], scores, neg_fill))

    def attend_block(block_index):
        first_row, allowed = block_inputs(block_index)

        def attend_head_group(group_index):
            query_head_rows, key_group, value_group, scores = group_scores(
                query_rotated, group_index, allowed
            )
            row_top = jnp.max(scores, axis=2, keepdims=True)
            powers = jnp.exp(scores - row_top)
            exp_total = jnp.sum(powers, axis=2, keepdims=True)
            attn_probs = (powers / exp_total).astype(jnp.bfloat16)
            weighted_values = jnp.einsum(
                "hqk,kd->qhd", attn_probs, value_group, preferred_element_type=jnp.float32
            )
            return (
                weighted_values.reshape(block_rows, group_head_width),
                (row_top + jnp.log(exp_total))[:, :, 0],
            )

        weighted_value_rows, logsumexp_rows = lax.map(
            attend_head_group, jnp.arange(KEY_VALUE_HEADS, dtype=jnp.int32)
        )
        return (
            jnp.transpose(weighted_value_rows, (1, 0, 2)).reshape(block_rows, query_width),
            logsumexp_rows,
        )

    mixed_blocks, log_blocks = lax.map(attend_block, jnp.arange(block_count, dtype=jnp.int32))
    attn_rows = mixed_blocks.reshape(query_rows, query_width).astype(jnp.bfloat16)
    attn_tokens = to_tokens(attn_rows)
    attn_share = col_sums(jnp.dot(attn_tokens, out_rows, preferred_element_type=jnp.float32))
    residual = layer_input.astype(jnp.float32) + attn_share
    inv_two = lax.rsqrt(jnp.mean(residual * residual, axis=1, keepdims=True) + eps)
    normed_two = residual * inv_two
    mlp_in = widen((normed_two * mlp_gain_float).astype(jnp.bfloat16))
    gate_act = jnp.dot(mlp_in, gate_cols, preferred_element_type=jnp.float32)
    up_act = jnp.dot(mlp_in, up_cols, preferred_element_type=jnp.float32)
    hidden = (jax.nn.silu(gate_act) * up_act).astype(jnp.bfloat16)
    mlp_share = col_sums(jnp.dot(hidden, down_rows, preferred_element_type=jnp.float32))
    layer_output = (residual + mlp_share).astype(jnp.bfloat16)
    grad_float = grad_output.astype(jnp.float32)
    grad_full = widen(grad_output)
    grad_down = jnp.einsum("tf,td->fd", hidden, grad_full, preferred_element_type=jnp.float32)
    grad_hidden = jnp.einsum("td,fd->tf", grad_full, down_rows, preferred_element_type=jnp.float32)
    gate_sigmoid = jax.nn.sigmoid(gate_act)
    grad_gate_act = (
        grad_hidden * up_act * gate_sigmoid * (1.0 + gate_act * (1.0 - gate_sigmoid))
    ).astype(jnp.bfloat16)
    grad_up_act = (grad_hidden * gate_act * gate_sigmoid).astype(jnp.bfloat16)
    grad_gate = jnp.einsum("td,tf->df", mlp_in, grad_gate_act, preferred_element_type=jnp.float32)
    grad_up = jnp.einsum("td,tf->df", mlp_in, grad_up_act, preferred_element_type=jnp.float32)
    grad_mlp_share = col_sums(
        jnp.einsum("tf,df->td", grad_gate_act, gate_cols, preferred_element_type=jnp.float32)
        + jnp.einsum("tf,df->td", grad_up_act, up_cols, preferred_element_type=jnp.float32)
    )
    scaled_two = grad_mlp_share * mlp_gain_float
    inner_two = jnp.mean(scaled_two * normed_two, axis=1, keepdims=True)
    grad_residual = grad_float + inv_two * (scaled_two - normed_two * inner_two)
    grad_mlp_gain = jnp.sum(grad_mlp_share * normed_two, axis=0)
    grad_branch = grad_residual.astype(jnp.bfloat16)
    grad_attn_full = widen(grad_branch)
    grad_out_weight = jnp.einsum(
        "tq,td->qd", attn_tokens, grad_attn_full, preferred_element_type=jnp.float32
    )
    grad_mixture = to_rows(
        jnp.einsum(
            "td,qd->tq", grad_attn_full, out_rows, preferred_element_type=jnp.float32
        ).astype(jnp.bfloat16)
    )

    def back_block(carried_state, scan_items):
        block_index, block_log_total = scan_items
        first_row, allowed = block_inputs(block_index)

        def backward_head_group(inner_acc, group_items):
            group_index, log_group = group_items
            keys_acc, values_acc = inner_acc
            query_head_rows, key_group, value_group, scores = group_scores(
                query_rotated, group_index, allowed
            )
            attn_probs = jnp.exp(scores - log_group[:, :, None])
            grad_heads = lax.dynamic_slice_in_dim(
                grad_mixture, group_index * group_head_width, group_head_width, 1
            ).reshape(block_rows, heads_per_group, HEAD_SIZE_DIM)
            grad_probs = jnp.einsum(
                "qhd,kd->hqk", grad_heads, value_group, preferred_element_type=jnp.float32
            )
            value_piece = jnp.einsum(
                "hqk,qhd->kd",
                attn_probs.astype(jnp.bfloat16),
                grad_heads,
                preferred_element_type=jnp.float32,
            )
            inner_dot = jnp.sum(attn_probs * grad_probs, axis=2, keepdims=True)
            grad_scores = (attn_probs * (grad_probs - inner_dot)).astype(jnp.bfloat16)
            query_piece = jnp.einsum(
                "hqk,kd->qhd", grad_scores, key_group, preferred_element_type=jnp.float32
            ).reshape(block_rows, group_head_width)
            key_piece = jnp.einsum(
                "hqk,qhd->kd", grad_scores, query_head_rows, preferred_element_type=jnp.float32
            )
            column = group_index * HEAD_SIZE_DIM
            keys_acc = lax.dynamic_update_slice_in_dim(
                keys_acc,
                lax.dynamic_slice_in_dim(keys_acc, column, HEAD_SIZE_DIM, 1) + key_piece,
                column,
                1,
            )
            values_acc = lax.dynamic_update_slice_in_dim(
                values_acc,
                lax.dynamic_slice_in_dim(values_acc, column, HEAD_SIZE_DIM, 1) + value_piece,
                column,
                1,
            )
            return ((keys_acc, values_acc), query_piece)

        carried_state, query_pieces = lax.scan(
            backward_head_group,
            carried_state,
            (jnp.arange(KEY_VALUE_HEADS, dtype=jnp.int32), block_log_total),
        )
        return (
            carried_state,
            jnp.transpose(query_pieces, (1, 0, 2)).reshape(block_rows, query_width),
        )

    zeros_kv = jnp.zeros((token_rows, key_all.shape[1]), jnp.float32)
    (grad_keys, grad_values), query_blocks = lax.scan(
        back_block, (zeros_kv, zeros_kv), (jnp.arange(block_count, dtype=jnp.int32), log_blocks)
    )
    grad_query_rot = query_blocks.reshape(query_rows, query_width)
    grad_query_raw = to_tokens(
        rotary_back(grad_query_rot * score_scale, query_cos, query_sin, HEAD_SIZE_DIM).astype(
            jnp.bfloat16
        )
    )
    grad_key_part = rotary_back(grad_keys, key_cos, key_sin, HEAD_SIZE_DIM)
    grad_key_sum, grad_value_sum = (
        lax.psum_scatter(grad_key_part, "col", scatter_dimension=1, tiled=True),
        lax.psum_scatter(grad_values, "col", scatter_dimension=1, tiled=True),
    )
    grad_key_raw = grad_key_sum.astype(jnp.bfloat16)
    grad_value_raw = grad_value_sum.astype(jnp.bfloat16)
    grad_query = jnp.einsum(
        "td,tq->dq", attn_in, grad_query_raw, preferred_element_type=jnp.float32
    )
    grad_key = jnp.einsum("td,tq->dq", attn_in, grad_key_raw, preferred_element_type=jnp.float32)
    grad_value = jnp.einsum(
        "td,tq->dq", attn_in, grad_value_raw, preferred_element_type=jnp.float32
    )
    grad_attn_share = col_sums(
        jnp.einsum("tq,dq->td", grad_query_raw, query_cols, preferred_element_type=jnp.float32)
        + jnp.einsum("tq,dq->td", grad_key_raw, key_cols, preferred_element_type=jnp.float32)
        + jnp.einsum("tq,dq->td", grad_value_raw, value_cols, preferred_element_type=jnp.float32)
    )
    own_float = layer_input.astype(jnp.float32)
    inv_one = lax.rsqrt(jnp.mean(own_float * own_float, axis=1, keepdims=True) + eps)
    normed_one = own_float * inv_one
    scaled_one = grad_attn_share * attn_gain_float
    inner_one = jnp.mean(scaled_one * normed_one, axis=1, keepdims=True)
    grad_input = (grad_residual + inv_one * (scaled_one - normed_one * inner_one)).astype(
        jnp.bfloat16
    )
    grad_attn_gain = jnp.sum(grad_attn_share * normed_one, axis=0)
    weight_sums = (
        lax.psum_scatter(grad_query, "row", scatter_dimension=0, tiled=True),
        lax.psum_scatter(grad_key, "row", scatter_dimension=0, tiled=True),
        lax.psum_scatter(grad_value, "row", scatter_dimension=0, tiled=True),
        lax.psum_scatter(grad_out_weight, "row", scatter_dimension=1, tiled=True),
        lax.psum_scatter(grad_gate, "row", scatter_dimension=0, tiled=True),
        lax.psum_scatter(grad_up, "row", scatter_dimension=0, tiled=True),
        lax.psum_scatter(grad_down, "row", scatter_dimension=1, tiled=True),
    )
    gain_sums = lax.psum((grad_attn_gain, grad_mlp_gain), ("row", "col"))
    return (
        layer_output,
        grad_input,
        gain_sums[0],
        gain_sums[1],
        weight_sums[0],
        weight_sums[1],
        weight_sums[2],
        weight_sums[3],
        weight_sums[4],
        weight_sums[5],
        weight_sums[6],
    )


def solution(mesh):
    in_specs = (
        P(("row", "col"), None),
        P(),
        P(),
        P("row", "col"),
        P("row", "col"),
        P("row", "col"),
        P("col", "row"),
        P("row", "col"),
        P("row", "col"),
        P("col", "row"),
        P("row"),
        P("row"),
        P(("row", "col"), None),
    )
    out_specs = (
        P(("row", "col"), None),
        P(("row", "col"), None),
        P(),
        P(),
        P("row", "col"),
        P("row", "col"),
        P("row", "col"),
        P("col", "row"),
        P("row", "col"),
        P("row", "col"),
        P("col", "row"),
    )
    return jax.shard_map(shards, mesh=mesh, in_specs=in_specs, out_specs=out_specs, check_vma=False)
```

profile of v0, /device:TPU:0, one launch (start us, length us, event | category | flops | bytes accessed | tf_op | source)
XLA Modules:
  0.0 1523.2 jit_solution(14034235379282888117)
XLA Ops:
  14.5 24.8 %all_gather.42 = bf16[1152,192]{1,0:T(8,128)(2,1)S(1)} all-gather(bf16[72,192]{1,0:T(8,128)(2,1)S(1)} %copy-done.33), channel_id=1, replica_groups=mesh['row'=16,'col'=2] {'row'}, dimensions={0}, use_global_device_ids=true | all-gather | bytes 470016 | tf_op jit(solution)/shard_map/all_gather | solution.py:93
  39.4 19.0 %all_gather.40 = bf16[1152,192]{1,0:T(8,128)(2,1)S(1)} all-gather(bf16[72,192]{1,0:T(8,128)(2,1)S(1)} %copy-done.34), channel_id=1, replica_groups=mesh['row'=16,'col'=2] {'row'}, dimensions={0}, use_global_device_ids=true | all-gather | bytes 470016 | tf_op jit(solution)/shard_map/all_gather | solution.py:94
  62.2 12.0 all_gather.43
  76.2 11.4 all_gather.41
  115.5 11.3 fusion.64
  126.8 62.2 %while.50 = (s32[]{:T(128)}, bf16[6,512,192]{1,2,0:T(8,128)(2,1)S(1)}, f32[6,3,512]{2,1,0:T(4,128)}, s32[6]{0:T(128)S(1)}, bf16[1024,384]{0,1:T(8,128)(2,1)}, /*...) while((s32[]{:T(128)}, ...), condition=%wide.region_6.7_spmd.clone.clone, body=%wide.region_3.6_spmd.clone.sunk.clone | while | flops 418380288 | bytes 22477056 | solution.py:168
  189.0 17.3 %all_to_all.64 = bf16[512,2,576]{0,2,1:T(8,128)(2,1)S(1)} all-to-all(bf16[512,2,576]{0,2,1:T(8,128)(2,1)S(1)} %bitcast.276), channel_id=1, replica_groups=mesh['row'=16,'col'=2] {'col'}, dimensions={1} | all-to-all | bytes 2359296 | tf_op jit(solution)/shard_map/all_to_all | solution.py:53
  214.1 56.8 %reduce-scatter.18.cloned.1.call-done = f32[512,1152]{1,0:T(8,128)} async-done(((f32[1024,1152]{1,0:T(8,128)}), f32[512,1152]{1,0:T(8,128)}) %reduce-scatter.18.cloned.1.call-update) | async-done | bytes 2359312 | tf_op jit(solution)/shard_map/reduce_scatter | solution.py:57
  277.9 42.6 %all-gather.20.cloned.1.call-done = bf16[1152,1536]{1,0:T(8,128)(2,1)} async-done(((bf16[72,1536]{1,0:T(8,128)(2,1)}), bf16[1152,1536]{1,0:T(8,128)(2,1)}) %all-gather.20.cloned.1.call-update) | async-done | bytes 3538960 | tf_op jit(solution)/shard_map/all_gather | solution.py:97
  320.5 37.1 %all-gather.16.cloned.1.call-done = bf16[1024,1152]{1,0:T(8,128)(2,1)} async-done(((bf16[512,1152]{1,0:T(8,128)(2,1)}), bf16[1024,1152]{1,0:T(8,128)(2,1)}) %all-gather.16.cloned.1.call-update) | async-done | bytes 2359312 | tf_op jit(solution)/shard_map/all_gather | solution.py:61
  357.6 9.6 fusion.126
  367.3 40.2 %all-gather.18.cloned.1.call-done = bf16[1152,1536]{1,0:T(8,128)(2,1)} async-done(((bf16[72,1536]{1,0:T(8,128)(2,1)}), bf16[1152,1536]{1,0:T(8,128)(2,1)}) %all-gather.18.cloned.1.call-update) | async-done | bytes 3538960 | tf_op jit(solution)/shard_map/all_gather | solution.py:96
  407.4 9.7 fusion.125
  417.1 27.0 %all-gather.24.cloned.1.call-done = bf16[1024,1152]{1,0:T(8,128)(2,1)} async-done(((bf16[512,1152]{1,0:T(8,128)(2,1)}), bf16[1024,1152]{1,0:T(8,128)(2,1)}) %all-gather.24.cloned.1.call-update) | async-done | bytes 2359312 | tf_op jit(solution)/shard_map/all_gather | solution.py:61
  444.1 49.8 %all-gather.22.cloned.1.call-done = bf16[1536,1152]{0,1:T(8,128)(2,1)} async-done(((bf16[1536,72]{0,1:T(8,128)(2,1)}), bf16[1536,1152]{0,1:T(8,128)(2,1)}) %all-gather.22.cloned.1.call-update) | async-done | bytes 3538960 | tf_op jit(solution)/shard_map/all_gather | solution.py:98
  493.9 12.5 multiply_convert_fusion
  516.8 59.1 %reduce-scatter.22.cloned.1.call-done = f32[512,1152]{1,0:T(8,128)} async-done(((f32[1024,1152]{1,0:T(8,128)}), f32[512,1152]{1,0:T(8,128)}) %reduce-scatter.22.cloned.1.call-update) | async-done | bytes 2359312 | tf_op jit(solution)/shard_map/reduce_scatter | solution.py:57
  581.8 36.2 %all-gather.26.cloned.1.call-done = bf16[1024,1152]{1,0:T(8,128)(2,1)} async-done(((bf16[512,1152]{1,0:T(8,128)(2,1)}), bf16[1024,1152]{1,0:T(8,128)(2,1)}) %all-gather.26.cloned.1.call-update) | async-done | bytes 2359312 | tf_op jit(solution)/shard_map/all_gather | solution.py:61
  627.7 15.1 all-to-all-done.2
  645.5 125.0 %while.51 = (s32[]{:T(128)}, f32[1024,384]{0,1:T(8,128)}, f32[1024,384]{0,1:T(8,128)}, f32[6,512,192]{1,2,0:T(8,128)}, s32[6]{0:T(128)S(1)}, /*index=5*/bf16[102...) while((s32[]{:T(128)}, f32[1024,384]{0,1:T(8,128)}, ...), condition=%wide.region_15.16_spmd.clone.clone, body=%wide.region_13.15_spmd.clone.sunk.clone | while | flops 1027209728 | bytes 55630144 | solution.py:265
  796.7 8.7 subtract_convert_fusion
  805.4 18.5 %all_to_all.65 = bf16[512,2,576]{0,2,1:T(8,128)(2,1)S(1)} all-to-all(bf16[512,2,576]{0,2,1:T(8,128)(2,1)S(1)} %subtract_convert_fusion), channel_id=1, replica_groups=mesh['row'=16,'col'=2] {'col'}, dimensions={1} | all-to-all | bytes 2359296 | tf_op jit(solution)/shard_map/all_to_all | solution.py:53
  846.7 9.4 fusion.127
  909.8 40.1 %all-reduce.2 = (f32[1152]{0:T(1024)}, f32[1152]{0:T(1024)}) all-reduce(f32[1152]{0:T(1024)} %get-tuple-element.251, f32[1152]{0:T(1024)} %get-tuple-element.249), channel_id=1, replica_groups=mesh['row'=16,'col'=2] {'row','col'}, use_global_device_ids=true, to_apply=%region_21.22 | all-reduce | flops 2304 | bytes 18432 | tf_op jit(solution)/shard_map/psum | solution.py:322
  951.1 19.2 %reduce-scatter.20.cloned.1.call-done = f32[512,1152]{1,0:T(8,128)} async-done(((f32[1024,1152]{1,0:T(8,128)}), f32[512,1152]{1,0:T(8,128)}) %reduce-scatter.20.cloned.1.call-update) | async-done | bytes 2359312 | tf_op jit(solution)/shard_map/reduce_scatter | solution.py:57
  975.4 89.2 %reduce-scatter.38.cloned.1.call-done = f32[1536,72]{0,1:T(8,128)} async-done(((f32[1536,1152]{0,1:T(8,128)}), f32[1536,72]{0,1:T(8,128)}) %reduce-scatter.38.cloned.1.call-update) | async-done | bytes 442384 | tf_op jit(solution)/shard_map/reduce_scatter | solution.py:320
  1064.7 94.5 %reduce-scatter.36.cloned.1.call-done = f32[72,1536]{1,0:T(8,128)} async-done(((f32[1152,1536]{1,0:T(8,128)}), f32[72,1536]{1,0:T(8,128)}) %reduce-scatter.36.cloned.1.call-update) | async-done | bytes 442384 | tf_op jit(solution)/shard_map/reduce_scatter | solution.py:319
  1159.2 94.0 %reduce-scatter.34.cloned.1.call-done = f32[72,1536]{1,0:T(8,128)} async-done(((f32[1152,1536]{1,0:T(8,128)}), f32[72,1536]{1,0:T(8,128)}) %reduce-scatter.34.cloned.1.call-update) | async-done | bytes 442384 | tf_op jit(solution)/shard_map/reduce_scatter | solution.py:318
  1253.3 69.9 %reduce-scatter.42.cloned.1.call-done = f32[576,72]{0,1:T(8,128)} async-done(((f32[576,1152]{0,1:T(8,128)}), f32[576,72]{0,1:T(8,128)}) %reduce-scatter.42.cloned.1.call-update) | async-done | bytes 165904
  1323.1 61.6 %reduce-scatter.32.cloned.1.call-done = f32[72,192]{1,0:T(8,128)} async-done(((f32[1152,192]{1,0:T(8,128)}), f32[72,192]{1,0:T(8,128)}) %reduce-scatter.32.cloned.1.call-update) | async-done | bytes 55312 | tf_op jit(solution)/shard_map/reduce_scatter | solution.py:316
  1384.8 61.8 %reduce-scatter.30.cloned.1.call-done = f32[72,192]{1,0:T(8,128)} async-done(((f32[1152,192]{1,0:T(8,128)}), f32[72,192]{1,0:T(8,128)}) %reduce-scatter.30.cloned.1.call-update) | async-done | bytes 55312 | tf_op jit(solution)/shard_map/reduce_scatter | solution.py:315
  1446.6 69.3 %reduce-scatter.40.cloned.1.call-done = f32[72,576]{1,0:T(8,128)} async-done(((f32[1152,576]{1,0:T(8,128)}), f32[72,576]{1,0:T(8,128)}) %reduce-scatter.40.cloned.1.call-update) | async-done | bytes 165904
  (358 shorter events, 363.0 us)
Async XLA Ops:
  7.2 51.2 %all-gather.10.cloned.1.call-start = ((), (), s32[]{:S(2)}) async-start(), calls=%async_computation.17 | async-start | bytes 3538944 | tf_op jit(solution)/shard_map/all_gather | solution.py:89
  8.0 82.0 %all-gather.12.cloned.1.call-start = ((), (), s32[]{:S(2)}) async-start(), calls=%async_computation.18 | async-start | bytes 1566720 | tf_op jit(solution)/shard_map/all_gather | solution.py:92
  8.7 197.8 %all-gather.14.cloned.1.call-start = ((), (), s32[]{:S(2)}) async-start(), calls=%async_computation.19 | async-start | bytes 1566720 | tf_op jit(solution)/shard_map/all_gather | solution.py:95
  13.9 47.0 %copy-start.24 = (f32[1024]{0:T(1024)}, f32[1024]{0:T(1024)S(1)}, u32[]{:S(2)}) copy-start(f32[1024]{0:T(1024)S(1)} %fusion.97) | copy-start | bytes 12292
  95.1 19.3 %all-to-all-start = ((bf16[2,512,576]{1,2,0:T(8,128)(2,1)}), bf16[2,512,576]{1,2,0:T(8,128)(2,1)S(1)}, u32[]{:S(2)}, u32[]{:S(2)}) async-start(bf16[2,512,576]{1,2,0:T(8,128)(2,1)} %bitcast.277), calls=%async_computation | async-start | bytes 2359296 | tf_op jit(solution)/shard_map/all_to_all | solution.py:49
  98.7 172.2 %reduce-scatter.18.cloned.1.call-start = ((), (), s32[]{:S(2)}) async-start(), calls=%async_computation.20 | async-start | bytes 7077888 | tf_op jit(solution)/shard_map/reduce_scatter | solution.py:57
  212.8 58.1 %copy-start.7 = (bf16[512,1152]{1,0:T(8,128)(2,1)S(1)}, bf16[512,1152]{1,0:T(8,128)(2,1)}, u32[]{:S(2)}) copy-start(bf16[512,1152]{1,0:T(8,128)(2,1)} %param.17) | copy-start | bytes 3538948
  212.8 107.7 %all-gather.20.cloned.1.call-start = ((), (), s32[]{:S(2)}) async-start(), calls=%async_computation.23 | async-start | bytes 3760128 | tf_op jit(solution)/shard_map/all_gather | solution.py:97
  213.4 144.2 %all-gather.16.cloned.1.call-start = ((), (), s32[]{:S(2)}) async-start(), calls=%async_computation.21 | async-start | bytes 3538944 | tf_op jit(solution)/shard_map/all_gather | solution.py:61
  273.7 305.2 %copy-start.1 = (f32[512,1152]{1,0:T(8,128)}, f32[512,1152]{1,0:T(8,128)S(1)}, u32[]{:S(2)}) copy-start(f32[512,1152]{1,0:T(8,128)S(1)} %get-tuple-element.306) | copy-start | bytes 7077892
  275.3 132.2 %all-gather.18.cloned.1.call-start = ((), (), s32[]{:S(2)}) async-start(), calls=%async_computation.22 | async-start | bytes 3760128 | tf_op jit(solution)/shard_map/all_gather | solution.py:96
  276.0 168.1 %all-gather.24.cloned.1.call-start = ((), (), s32[]{:S(2)}) async-start(), calls=%async_computation.26 | async-start | bytes 3538944 | tf_op jit(solution)/shard_map/all_gather | solution.py:61
  276.8 217.1 %all-gather.22.cloned.1.call-start = ((), (), s32[]{:S(2)}) async-start(), calls=%async_computation.24 | async-start | bytes 3760128 | tf_op jit(solution)/shard_map/all_gather | solution.py:98
  277.5 298.4 %reduce-scatter.22.cloned.1.call-start = ((), (), s32[]{:S(2)}) async-start(), calls=%async_computation.27 | async-start | bytes 7077888 | tf_op jit(solution)/shard_map/reduce_scatter | solution.py:57
  516.7 62.8 %copy-start.9 = (bf16[512,1152]{1,0:T(8,128)(2,1)S(1)}, bf16[512,1152]{1,0:T(8,128)(2,1)}, u32[]{:S(2)}) copy-start(bf16[512,1152]{1,0:T(8,128)(2,1)} %param.29) | copy-start | bytes 3538948
  516.7 101.3 %all-gather.26.cloned.1.call-start = ((), (), s32[]{:S(2)}) async-start(), calls=%async_computation.28 | async-start | bytes 3538944 | tf_op jit(solution)/shard_map/all_gather | solution.py:61
  623.0 19.8 %all-to-all-start.2 = ((bf16[2,512,576]{1,2,0:T(8,128)(2,1)}), bf16[2,512,576]{1,2,0:T(8,128)(2,1)}, u32[]{:S(2)}, u32[]{:S(2)}) async-start(bf16[2,512,576]{1,2,0:T(8,128)(2,1)} %bitcast.162), calls=%async_computation.5 | async-start | bytes 2359296 | tf_op jit(solution)/shard_map/all_to_all | solution.py:49
  627.4 201.0 %reduce-scatter.24.cloned.1.call-start = ((), (), s32[]{:S(2)}) async-start(), calls=%async_computation.29 | async-start | bytes 2359296 | tf_op jit(solution)/shard_map/reduce_scatter | solution.py:287
  645.5 125.0 %copy-start.26 = (f32[1024]{0:T(1024)S(1)}, f32[1024]{0:T(1024)}, u32[]{:S(2)}) copy-start(f32[1024]{0:T(1024)} %copy-done.24) | copy-start | bytes 12292
  645.5 125.0 %copy-start.36 = (f32[384]{0:T(512)S(1)}, f32[384]{0:T(512)}, u32[]{:S(2)}) copy-start(f32[384]{0:T(512)} %fusion.100) | copy-start | bytes 4612
  785.3 55.7 %reduce-scatter.26.cloned.1.call-start = ((), (), s32[]{:S(2)}) async-start(), calls=%async_computation.30 | async-start | bytes 2359296 | tf_op jit(solution)/shard_map/reduce_scatter | solution.py:288
  794.4 112.4 %reduce-scatter.28.cloned.1.call-start = ((), (), s32[]{:S(2)}) async-start(), calls=%async_computation.31 | async-start | bytes 7077888 | tf_op jit(solution)/shard_map/reduce_scatter | solution.py:57
  846.7 123.7 %reduce-scatter.20.cloned.1.call-start = ((), (), s32[]{:S(2)}) async-start(), calls=%async_computation.25 | async-start | bytes 7077888 | tf_op jit(solution)/shard_map/reduce_scatter | solution.py:57
  856.1 208.6 %reduce-scatter.38.cloned.1.call-start = ((), (), s32[]{:S(2)}) async-start(), calls=%async_computation.36 | async-start | bytes 7520256 | tf_op jit(solution)/shard_map/reduce_scatter | solution.py:320
  865.4 293.8 %reduce-scatter.36.cloned.1.call-start = ((), (), s32[]{:S(2)}) async-start(), calls=%async_computation.35 | async-start | bytes 7520256 | tf_op jit(solution)/shard_map/reduce_scatter | solution.py:319
  874.7 378.6 %reduce-scatter.34.cloned.1.call-start = ((), (), s32[]{:S(2)}) async-start(), calls=%async_computation.34 | async-start | bytes 7520256 | tf_op jit(solution)/shard_map/reduce_scatter | solution.py:318
  882.6 440.5 %reduce-scatter.42.cloned.1.call-start = ((), (), s32[]{:S(2)}) async-start(), calls=%async_computation.38 | async-start | bytes 3133440
  889.3 495.4 %reduce-scatter.32.cloned.1.call-start = ((), (), s32[]{:S(2)}) async-start(), calls=%async_computation.33 | async-start | bytes 1253376 | tf_op jit(solution)/shard_map/reduce_scatter | solution.py:316
  894.2 552.4 %reduce-scatter.30.cloned.1.call-start = ((), (), s32[]{:S(2)}) async-start(), calls=%async_computation.32 | async-start | bytes 1253376 | tf_op jit(solution)/shard_map/reduce_scatter | solution.py:315
  897.5 618.4 %reduce-scatter.40.cloned.1.call-start = ((), (), s32[]{:S(2)}) async-start(), calls=%async_computation.37 | async-start | bytes 3133440
  901.6 68.7 %copy-start.2 = (f32[512,1152]{1,0:T(8,128)S(1)}, f32[512,1152]{1,0:T(8,128)}, u32[]{:S(2)}) copy-start(f32[512,1152]{1,0:T(8,128)} %copy-done.1) | copy-start | bytes 7077892
  901.6 68.7 %copy-start.23 = (f32[1152]{0:T(1024)S(1)}, f32[1152]{0:T(1024)}, u32[]{:S(2)}) copy-start(f32[1152]{0:T(1024)} %convert_element_type.142) | copy-start | bytes 13828
  (51 other events, 326.2 us)
Sparse Core Ops, SparseCore 0:
  9.6 38.7 all-gather.9
  50.6 39.3 all-gather.11
  92.1 38.1 all-gather.13
  212.9 57.8 reduce-scatter.17
  273.3 47.1 all-gather.19
  322.5 35.0 all-gather.15
  360.2 47.1 all-gather.17
  409.0 35.0 all-gather.23
  446.7 47.1 all-gather.21
  516.8 58.9 reduce-scatter.21
  582.0 36.0 all-gather.25
  785.4 26.4 reduce-scatter.23
  814.2 26.7 reduce-scatter.25
  846.8 59.9 reduce-scatter.27
  909.1 61.2 reduce-scatter.19
  974.8 89.8 reduce-scatter.37
  1069.6 89.5 reduce-scatter.35
  1163.7 89.5 reduce-scatter.33
  1258.3 64.8 reduce-scatter.41
  1327.6 57.0 reduce-scatter.31
  1389.4 57.1 reduce-scatter.29
  1451.6 64.2 reduce-scatter.39
where the time goes:
time: 1530 us; the launch traced here: 1520 us
  waiting for transfers between devices  949 us (62%)
  matrix products  228 us (15%)
  blocking collectives  143 us (9%)
  other arithmetic  115 us (8%)
  local copies, waits for them, and re-layouts  45.7 us (3%)
  loops' own time  16.1 us (1%)
  between operations  16.1 us (1%)
    unnamed x24, waiting for transfers between devices  144 us
    reduce_scatter x4, waiting for transfers between devices, col_sums(): return lax.psum_scatter(values, 'col', scatter_dimension=0, tiled=True)  139 us
    all_gather x3, waiting for transfers between devices, widen(): return lax.all_gather(values, 'col', axis=0, tiled=True)  100 us
    reduce_scatter x1, waiting for transfers between devices, shards(): lax.psum_scatter(grad_up, 'row', scatter_dimension=0, tiled=True)  94.5 us
    reduce_scatter x1, waiting for transfers between devices, shards(): lax.psum_scatter(grad_gate, 'row', scatter_dimension=0, tiled=True)  94 us
    reduce_scatter x1, waiting for transfers between devices, shards(): lax.psum_scatter(grad_down, 'row', scatter_dimension=1, tiled=True)  89.2 us
    reduce_scatter x1, waiting for transfers between devices, shards(): lax.psum_scatter(grad_key, 'row', scatter_dimension=0, tiled=True)  61.8 us
    reduce_scatter x1, waiting for transfers between devices, shards(): lax.psum_scatter(grad_value, 'row', scatter_dimension=0, tiled=True)  61.6 us
  transfers between devices with their start and end apart: 24, of which 21 were waited for; matrix products, arithmetic and copies ran while one was open for 13% of the time, Pallas kernels for 0%

commit v1 on v0

--- a/solution.py
+++ b/solution.py
@@ -3,6 +3,7 @@
 import jax.numpy as jnp
 from jax import lax
 from jax.sharding import PartitionSpec as P
+from jax.lax import axis_index, axis_size, ppermute
 
 QUERY_HEADS = 18
 KEY_VALUE_HEADS = 6
@@ -12,6 +13,30 @@
 neg_fill = -1e30
 
 
+def sheet_list(local_x, axis_no):
+    parts_out = list(local_x.shape[1:])
+    parts_out[axis_no] *= local_x.shape[0]
+    return jnp.moveaxis(local_x, 0, axis_no).reshape(parts_out)
+
+
+def skins_store(row_data, device_axis):
+    t_next = row_data[None]
+    n_peers_all = axis_size(device_axis)
+    for d in range(n_peers_all.bit_length() - 1):
+        small = 1 << d
+        b_next = ppermute(
+            t_next, axis_name=device_axis, perm=[(ii, ii ^ small) for ii in range(n_peers_all)]
+        )
+        newest = jnp.stack([t_next, b_next])
+        placed = axis_index(device_axis) >> d & 1
+        t_next = jnp.where(placed == 0, newest, newest[::-1]).reshape(-1, *row_data.shape)
+    return t_next
+
+
+def raise_ladders_on(obj, tile_in, dim_no):
+    return sheet_list(skins_store(obj, tile_in), dim_no)
+
+
 def rotate_half(values, head_size):
     lane_index = jnp.arange(values.shape[-1], dtype=jnp.int32) % head_size
     forward_roll = jnp.roll(values, -(head_size // 2), axis=-1)
@@ -58,7 +83,7 @@
 
 
 def widen(values):
-    return lax.all_gather(values, "col", axis=0, tiled=True)
+    return raise_ladders_on(values, "col", 0)
 
 
 def shards(

time: 1530 us -> 1460 us (0.954)
  waiting for transfers between devices: 949 us -> 876 us
  matrix products: 228 us -> 212 us
    all_gather x3 -> x0, waiting for transfers between devices: 100 us -> none  [widen(): return lax.all_gather(values, 'col', axis=0, tiled=True)]
    reduce_scatter x4, waiting for transfers between devices: 139 us -> 201 us  [col_sums(): return lax.psum_scatter(values, 'col', scatter_dimension=0, tiled=True)]
    ppermute x0 -> x3, waiting for transfers between devices: none -> 53.1 us  [skins_store(): ppermute(t_next, axis_name=device_axis, perm=[(ii, ii ^ small) for ii in...]
    reduce_scatter x1, waiting for transfers between devices: 94 us -> 48.4 us  [shards(): lax.psum_scatter(grad_gate, 'row', scatter_dimension=0, tiled=True)]
    all_gather x1, waiting for transfers between devices: 40.2 us -> 10.6 us  [shards(): lax.all_gather(gate_weight, 'row', axis=0, tiled=True)]
    unnamed x24 -> x21, waiting for transfers between devices: 144 us -> 143 us
  transfers between devices with their start and end apart: 24 -> 24, of which waited for: 21 -> 20; matrix products, arithmetic and copies ran while one was open for 13% -> 14% of each run, Pallas kernels for 0% -> 0%
where the time goes in v1:
time: 1460 us; the launch traced here: 1450 us
  waiting for transfers between devices  876 us (60%)
  matrix products  212 us (15%)
  blocking collectives  143 us (10%)
  other arithmetic  122 us (8%)
  local copies, waits for them, and re-layouts  53.9 us (4%)
  loops' own time  16.2 us (1%)
  between operations  15.8 us (1%)
    reduce_scatter x4, waiting for transfers between devices, col_sums(): return lax.psum_scatter(values, 'col', scatter_dimension=0, tiled=True)  201 us
    unnamed x21, waiting for transfers between devices  143 us
    reduce_scatter x1, waiting for transfers between devices, shards(): lax.psum_scatter(grad_up, 'row', scatter_dimension=0, tiled=True)  94.6 us
    reduce_scatter x1, waiting for transfers between devices, shards(): lax.psum_scatter(grad_down, 'row', scatter_dimension=1, tiled=True)  94 us
    reduce_scatter x1, waiting for transfers between devices, shards(): lax.psum_scatter(grad_value, 'row', scatter_dimension=0, tiled=True)  61.6 us
    reduce_scatter x1, waiting for transfers between devices, shards(): lax.psum_scatter(grad_key, 'row', scatter_dimension=0, tiled=True)  61.5 us
    ppermute x3, waiting for transfers between devices, skins_store(): ppermute(t_next, axis_name=device_axis, perm=[(ii, ii ^ small) for ii in...  53.1 us
    reduce_scatter x1, waiting for transfers between devices, shards(): lax.psum_scatter(grad_gate, 'row', scatter_dimension=0, tiled=True)  48.4 us
  transfers between devices with their start and end apart: 24, of which 20 were waited for; matrix products, arithmetic and copies ran while one was open for 14% of the time, Pallas kernels for 0%

profile of v1, /device:TPU:0, one launch (start us, length us, event | category | flops | bytes accessed | tf_op | source)
XLA Modules:
  0.0 1449.4 jit_solution(1018670565512623835)
XLA Ops:
  16.0 24.8 %all_gather.33 = bf16[1152,192]{1,0:T(8,128)(2,1)S(1)} all-gather(bf16[72,192]{1,0:T(8,128)(2,1)S(1)} %copy-done.41), channel_id=1, replica_groups=mesh['row'=16,'col'=2] {'row'}, dimensions={0}, use_global_device_ids=true | all-gather | bytes 470016 | tf_op jit(solution)/shard_map/all_gather | solution.py:118
  40.9 19.0 %all_gather.31 = bf16[1152,192]{1,0:T(8,128)(2,1)S(1)} all-gather(bf16[72,192]{1,0:T(8,128)(2,1)S(1)} %copy-done.42), channel_id=1, replica_groups=mesh['row'=16,'col'=2] {'row'}, dimensions={0}, use_global_device_ids=true | all-gather | bytes 470016 | tf_op jit(solution)/shard_map/all_gather | solution.py:119
  63.7 12.0 all_gather.34
  77.6 11.2 all_gather.32
  115.5 11.3 fusion.64
  126.8 55.4 %while.50 = (s32[]{:T(128)}, bf16[6,512,192]{1,2,0:T(8,128)(2,1)}, f32[6,3,512]{2,1,0:T(4,128)}, s32[6]{0:T(128)S(1)}, bf16[1024,384]{0,1:T(8,128)(2,1)S(1)}, /*...) while((s32[]{:T(128)}, bf16[6,512,192]{1,2,0:T(8,128)(2,1)}, ...), condition=%wide.region_6.7_spmd.clone.clone, body=%wide.region_3.6_spmd.clone.sunk.clone | while | flops 418380288 | bytes 22482160 | solution.py:193
  182.1 18.5 %all_to_all.64 = bf16[512,2,576]{0,2,1:T(8,128)(2,1)S(1)} all-to-all(bf16[512,2,576]{0,2,1:T(8,128)(2,1)} %bitcast.292), channel_id=1, replica_groups=mesh['row'=16,'col'=2] {'col'}, dimensions={1} | all-to-all | bytes 2359296 | tf_op jit(solution)/shard_map/all_to_all | solution.py:78
  210.2 77.8 %reduce-scatter.18.cloned.1.call-done = f32[512,1152]{1,0:T(8,128)} async-done(((f32[1024,1152]{1,0:T(8,128)}), f32[512,1152]{1,0:T(8,128)}) %reduce-scatter.18.cloned.1.call-update) | async-done | bytes 2359312 | tf_op jit(solution)/shard_map/reduce_scatter | solution.py:82
  294.6 25.7 %collective-permute-done = bf16[1,512,1152]{2,1,0:T(8,128)(2,1)} collective-permute-done((bf16[1,512,1152]{2,1,0:T(8,128)(2,1)}, bf16[1,512,1152]{2,1,0:T(8,128)(2,1)}, u32[]{:S(2)}, u32[]{:S(2)}) %collective-permute-start) | collective-permute-done | bytes 1179680 | tf_op jit(solution)/shard_map/ppermute | solution.py:27
  325.0 10.6 all-gather.13.cloned.1.call-done
  335.5 9.6 fusion.126
  345.1 39.0 %all-gather.15.cloned.1.call-done = bf16[1152,1536]{1,0:T(8,128)(2,1)} async-done(((bf16[72,1536]{1,0:T(8,128)(2,1)}), bf16[1152,1536]{1,0:T(8,128)(2,1)}) %all-gather.15.cloned.1.call-update) | async-done | bytes 3538960 | tf_op jit(solution)/shard_map/all_gather | solution.py:122
  384.1 9.6 fusion.127
  393.8 39.1 %all-gather.17.cloned.1.call-done = bf16[1536,1152]{0,1:T(8,128)(2,1)} async-done(((bf16[1536,72]{0,1:T(8,128)(2,1)}), bf16[1536,1152]{0,1:T(8,128)(2,1)}) %all-gather.17.cloned.1.call-update) | async-done | bytes 3538960 | tf_op jit(solution)/shard_map/all_gather | solution.py:123
  432.9 12.7 multiply_convert_fusion
  456.6 9.4 fusion.128
  466.0 49.2 %reduce-scatter.22.cloned.1.call-done = f32[512,1152]{1,0:T(8,128)} async-done(((f32[1024,1152]{1,0:T(8,128)}), f32[512,1152]{1,0:T(8,128)}) %reduce-scatter.22.cloned.1.call-update) | async-done | bytes 2359312 | tf_op jit(solution)/shard_map/reduce_scatter | solution.py:82
  518.0 59.5 %reduce-scatter.20.cloned.1.call-done = f32[512,1152]{1,0:T(8,128)} async-done(((f32[1024,1152]{1,0:T(8,128)}), f32[512,1152]{1,0:T(8,128)}) %reduce-scatter.20.cloned.1.call-update) | async-done | bytes 2359312 | tf_op jit(solution)/shard_map/reduce_scatter | solution.py:82
  582.5 27.4 %collective-permute-done.2 = bf16[1,512,1152]{2,1,0:T(8,128)(2,1)S(1)} collective-permute-done((bf16[1,512,1152]{2,1,0:T(8,128)(2,1)S(1)}, bf16[1,512,1152]{2,1,0:T(8,128)(2,1)S(1)}, u32[]{:S(2)}, u32[]{:S(2)}) %collective-permute-start.2) | collective-permute-done | bytes 1179680 | tf_op jit(solution)/shard_map/ppermute | solution.py:27
  618.2 14.1 all-to-all-done.2
  635.1 125.2 %while.51 = (s32[]{:T(128)}, f32[1024,384]{0,1:T(8,128)}, f32[1024,384]{0,1:T(8,128)}, f32[6,512,192]{1,2,0:T(8,128)}, s32[6]{0:T(128)S(1)}, /*index=5*/bf16[102...) while((s32[]{:T(128)}, f32[1024,384]{0,1:T(8,128)}, ...), condition=%wide.region_15.16_spmd.clone.clone, body=%wide.region_13.15_spmd.clone.sunk.clone | while | flops 1027209728 | bytes 67165064 | solution.py:290
  786.4 8.7 subtract_convert_fusion
  795.1 17.6 %all_to_all.65 = bf16[512,2,576]{0,2,1:T(8,128)(2,1)S(1)} all-to-all(bf16[512,2,576]{0,2,1:T(8,128)(2,1)S(1)} %subtract_convert_fusion), channel_id=1, replica_groups=mesh['row'=16,'col'=2] {'col'}, dimensions={1} | all-to-all | bytes 2359296 | tf_op jit(solution)/shard_map/all_to_all | solution.py:78
  882.0 14.7 %reduce-scatter.28.cloned.1.call-done = f32[512,1152]{1,0:T(8,128)} async-done(((f32[1024,1152]{1,0:T(8,128)}), f32[512,1152]{1,0:T(8,128)}) %reduce-scatter.28.cloned.1.call-update) | async-done | bytes 2359312 | tf_op jit(solution)/shard_map/reduce_scatter | solution.py:82
  899.6 39.7 %all-reduce.2 = (f32[1152]{0:T(1024)}, f32[1152]{0:T(1024)}) all-reduce(f32[1152]{0:T(1024)} %get-tuple-element.251, f32[1152]{0:T(1024)S(1)} %copy-done.43), channel_id=1, replica_groups=mesh['row'=16,'col'=2] {'row','col'}, use_global_device_ids=true, to_apply=%region_21.22 | all-reduce | flops 2304 | bytes 18432 | tf_op jit(solution)/shard_map/psum | solution.py:347
  943.3 48.4 %reduce-scatter.34.cloned.1.call-done = f32[72,1536]{1,0:T(8,128)} async-done(((f32[1152,1536]{1,0:T(8,128)}), f32[72,1536]{1,0:T(8,128)}) %reduce-scatter.34.cloned.1.call-update) | async-done | bytes 442384 | tf_op jit(solution)/shard_map/reduce_scatter | solution.py:343
  991.8 94.6 %reduce-scatter.36.cloned.1.call-done = f32[72,1536]{1,0:T(8,128)} async-done(((f32[1152,1536]{1,0:T(8,128)}), f32[72,1536]{1,0:T(8,128)}) %reduce-scatter.36.cloned.1.call-update) | async-done | bytes 442384 | tf_op jit(solution)/shard_map/reduce_scatter | solution.py:344
  1086.4 94.0 %reduce-scatter.38.cloned.1.call-done = f32[1536,72]{0,1:T(8,128)} async-done(((f32[1536,1152]{0,1:T(8,128)}), f32[1536,72]{0,1:T(8,128)}) %reduce-scatter.38.cloned.1.call-update) | async-done | bytes 442384 | tf_op jit(solution)/shard_map/reduce_scatter | solution.py:345
  1180.4 69.7 %reduce-scatter.42.cloned.1.call-done = f32[576,72]{0,1:T(8,128)} async-done(((f32[576,1152]{0,1:T(8,128)}), f32[576,72]{0,1:T(8,128)}) %reduce-scatter.42.cloned.1.call-update) | async-done | bytes 165904
  1250.0 61.5 %reduce-scatter.30.cloned.1.call-done = f32[72,192]{1,0:T(8,128)} async-done(((f32[1152,192]{1,0:T(8,128)}), f32[72,192]{1,0:T(8,128)}) %reduce-scatter.30.cloned.1.call-update) | async-done | bytes 55312 | tf_op jit(solution)/shard_map/reduce_scatter | solution.py:340
  1311.6 61.6 %reduce-scatter.32.cloned.1.call-done = f32[72,192]{1,0:T(8,128)} async-done(((f32[1152,192]{1,0:T(8,128)}), f32[72,192]{1,0:T(8,128)}) %reduce-scatter.32.cloned.1.call-update) | async-done | bytes 55312 | tf_op jit(solution)/shard_map/reduce_scatter | solution.py:341
  1373.2 69.3 %reduce-scatter.40.cloned.1.call-done = f32[72,576]{1,0:T(8,128)} async-done(((f32[1152,576]{1,0:T(8,128)}), f32[72,576]{1,0:T(8,128)}) %reduce-scatter.40.cloned.1.call-update) | async-done | bytes 165904
  (410 shorter events, 357.0 us)
Async XLA Ops:
  7.2 52.7 %copy-start.31 = (s32[1024]{0:T(1024)S(1)}, s32[1024]{0:T(1024)}, u32[]{:S(2)}) copy-start(s32[1024]{0:T(1024)} %param.28) | copy-start | bytes 12292
  7.2 52.8 %all-gather.7.cloned.1.call-start = ((), (), s32[]{:S(2)}) async-start(), calls=%async_computation.17 | async-start | bytes 3538944 | tf_op jit(solution)/shard_map/all_gather | solution.py:114
  8.0 82.0 %all-gather.9.cloned.1.call-start = ((), (), s32[]{:S(2)}) async-start(), calls=%async_computation.18 | async-start | bytes 1566720 | tf_op jit(solution)/shard_map/all_gather | solution.py:117
  8.7 192.1 %all-gather.11.cloned.1.call-start = ((), (), s32[]{:S(2)}) async-start(), calls=%async_computation.19 | async-start | bytes 1566720 | tf_op jit(solution)/shard_map/all_gather | solution.py:120
  13.0 77.0 %copy-start.37 = (f32[1152]{0:T(1024)}, f32[1152]{0:T(1024)S(1)}, u32[]{:S(2)}) copy-start(f32[1152]{0:T(1024)S(1)} %convert_element_type.125) | copy-start | bytes 13828
  95.0 19.3 %all-to-all-start = ((bf16[2,512,576]{1,2,0:T(8,128)(2,1)}), bf16[2,512,576]{1,2,0:T(8,128)(2,1)S(1)}, u32[]{:S(2)}, u32[]{:S(2)}) async-start(bf16[2,512,576]{1,2,0:T(8,128)(2,1)} %bitcast.179), calls=%async_computation | async-start | bytes 2359296 | tf_op jit(solution)/shard_map/all_to_all | solution.py:74
  98.7 189.3 %reduce-scatter.18.cloned.1.call-start = ((), (), s32[]{:S(2)}) async-start(), calls=%async_computation.20 | async-start | bytes 7077888 | tf_op jit(solution)/shard_map/reduce_scatter | solution.py:82
  207.0 81.0 %copy-start.7 = (bf16[512,1152]{1,0:T(8,128)(2,1)S(1)}, bf16[512,1152]{1,0:T(8,128)(2,1)}, u32[]{:S(2)}) copy-start(bf16[512,1152]{1,0:T(8,128)(2,1)} %param.17) | copy-start | bytes 3538948
  207.0 128.5 %all-gather.13.cloned.1.call-start = ((), (), s32[]{:S(2)}) async-start(), calls=%async_computation.21 | async-start | bytes 3760128 | tf_op jit(solution)/shard_map/all_gather | solution.py:121
  207.6 176.5 %all-gather.15.cloned.1.call-start = ((), (), s32[]{:S(2)}) async-start(), calls=%async_computation.22 | async-start | bytes 3760128 | tf_op jit(solution)/shard_map/all_gather | solution.py:122
  208.2 224.7 %all-gather.17.cloned.1.call-start = ((), (), s32[]{:S(2)}) async-start(), calls=%async_computation.23 | async-start | bytes 3760128 | tf_op jit(solution)/shard_map/all_gather | solution.py:123
  208.9 306.2 %reduce-scatter.22.cloned.1.call-start = ((), (), s32[]{:S(2)}) async-start(), calls=%async_computation.25 | async-start | bytes 7077888 | tf_op jit(solution)/shard_map/reduce_scatter | solution.py:82
  209.2 83.5 %collective-permute-start.1 = (bf16[1,512,1152]{2,1,0:T(8,128)(2,1)}, bf16[1,512,1152]{2,1,0:T(8,128)(2,1)}, u32[]{:S(2)}, u32[]{:S(2)}) collective-permute-start(bf16[1,512,1152]{2,1,0:T(8,128)(2,1)} %bitcast.13), channel_id=1, source_target_pairs={{0,1},{1,0},{2,3},{3,2},{4,5},{5,4},{6,7},{7,6},{8,9},{9,8},{10,11... | collective-permute-start | bytes 3538952 | tf_op jit(solution)/shard_map/ppermute | solution.py:27
  292.1 28.2 %collective-permute-start = (bf16[1,512,1152]{2,1,0:T(8,128)(2,1)}, bf16[1,512,1152]{2,1,0:T(8,128)(2,1)}, u32[]{:S(2)}, u32[]{:S(2)}) collective-permute-start(bf16[1,512,1152]{2,1,0:T(8,128)(2,1)} %get-tuple-element.319), channel_id=1, source_target_pairs={{0,1},{1,0},{2,3},{3,2},{4,5},{5,4},{6,7},{7,6},{8,9},{9,8},{10,11... | collective-permute-start | bytes 3538952 | tf_op jit(solution)/shard_map/ppermute | solution.py:27
  456.0 121.5 %reduce-scatter.20.cloned.1.call-start = ((), (), s32[]{:S(2)}) async-start(), calls=%async_computation.24 | async-start | bytes 7077888 | tf_op jit(solution)/shard_map/reduce_scatter | solution.py:82
  465.9 49.2 %copy-start.33 = (f32[1152]{0:T(1024)S(1)}, f32[1152]{0:T(1024)}, u32[]{:S(2)}) copy-start(f32[1152]{0:T(1024)} %convert_element_type.142) | copy-start | bytes 13828
  465.9 49.2 %copy-start.47 = (f32[512]{0:T(512)S(1)}, f32[512]{0:T(512)}, u32[]{:S(2)}) copy-start(f32[512]{0:T(512)} %copy-done.46) | copy-start | bytes 6148
  582.1 27.8 %collective-permute-start.2 = (bf16[1,512,1152]{2,1,0:T(8,128)(2,1)S(1)}, bf16[1,512,1152]{2,1,0:T(8,128)(2,1)S(1)}, u32[]{:S(2)}, u32[]{:S(2)}) collective-permute-start(bf16[1,512,1152]{2,1,0:T(8,128)(2,1)S(1)} %convert_bitcast_fusion), channel_id=1, source_target_pairs={{0,1},{1,0},{2,3},{3,2},{4,5},{5,4},{6,7},{7,6},{8,9},{9,8},{10,11... | collective-permute-start | bytes 3538952 | tf_op jit(solution)/shard_map/ppermute | solution.py:27
  614.4 18.0 %all-to-all-start.2 = ((bf16[2,512,576]{1,2,0:T(8,128)(2,1)}), bf16[2,512,576]{1,2,0:T(8,128)(2,1)S(1)}, u32[]{:S(2)}, u32[]{:S(2)}) async-start(bf16[2,512,576]{1,2,0:T(8,128)(2,1)} %bitcast.178), calls=%async_computation.5 | async-start | bytes 2359296 | tf_op jit(solution)/shard_map/all_to_all | solution.py:74
  618.0 200.4 %reduce-scatter.24.cloned.1.call-start = ((), (), s32[]{:S(2)}) async-start(), calls=%async_computation.26 | async-start | bytes 2359296 | tf_op jit(solution)/shard_map/reduce_scatter | solution.py:312
  635.1 125.2 %copy-start.36 = (f32[1024]{0:T(1024)S(1)}, f32[1024]{0:T(1024)}, u32[]{:S(2)}) copy-start(f32[1024]{0:T(1024)} %copy-done.34) | copy-start | bytes 12292
  635.1 125.2 %copy-start.45 = (f32[384]{0:T(512)S(1)}, f32[384]{0:T(512)}, u32[]{:S(2)}) copy-start(f32[384]{0:T(512)} %fusion.100) | copy-start | bytes 4612
  775.0 55.7 %reduce-scatter.26.cloned.1.call-start = ((), (), s32[]{:S(2)}) async-start(), calls=%async_computation.27 | async-start | bytes 2359296 | tf_op jit(solution)/shard_map/reduce_scatter | solution.py:313
  784.1 112.5 %reduce-scatter.28.cloned.1.call-start = ((), (), s32[]{:S(2)}) async-start(), calls=%async_computation.28 | async-start | bytes 7077888 | tf_op jit(solution)/shard_map/reduce_scatter | solution.py:82
  836.5 155.3 %reduce-scatter.34.cloned.1.call-start = ((), (), s32[]{:S(2)}) async-start(), calls=%async_computation.31 | async-start | bytes 7520256 | tf_op jit(solution)/shard_map/reduce_scatter | solution.py:343
  845.7 240.7 %reduce-scatter.36.cloned.1.call-start = ((), (), s32[]{:S(2)}) async-start(), calls=%async_computation.32 | async-start | bytes 7520256 | tf_op jit(solution)/shard_map/reduce_scatter | solution.py:344
  853.4 327.0 %reduce-scatter.38.cloned.1.call-start = ((), (), s32[]{:S(2)}) async-start(), calls=%async_computation.33 | async-start | bytes 7520256 | tf_op jit(solution)/shard_map/reduce_scatter | solution.py:345
  862.7 387.3 %reduce-scatter.42.cloned.1.call-start = ((), (), s32[]{:S(2)}) async-start(), calls=%async_computation.35 | async-start | bytes 3133440
  868.4 443.2 %reduce-scatter.30.cloned.1.call-start = ((), (), s32[]{:S(2)}) async-start(), calls=%async_computation.29 | async-start | bytes 1253376 | tf_op jit(solution)/shard_map/reduce_scatter | solution.py:340
  873.3 499.9 %reduce-scatter.32.cloned.1.call-start = ((), (), s32[]{:S(2)}) async-start(), calls=%async_computation.30 | async-start | bytes 1253376 | tf_op jit(solution)/shard_map/reduce_scatter | solution.py:341
  876.6 565.8 %reduce-scatter.40.cloned.1.call-start = ((), (), s32[]{:S(2)}) async-start(), calls=%async_computation.34 | async-start | bytes 3133440
  880.6 59.4 %copy-start.6 = (f32[512,1152]{1,0:T(8,128)S(1)}, f32[512,1152]{1,0:T(8,128)}, u32[]{:S(2)}) copy-start(f32[512,1152]{1,0:T(8,128)} %copy-done.5) | copy-start | bytes 7077892
  (75 other events, 440.0 us)
Sparse Core Ops, SparseCore 0:
  9.6 38.7 all-gather.6
  50.6 39.3 all-gather.8
  92.1 38.1 all-gather.10
  207.1 80.7 reduce-scatter.17
  290.3 45.1 all-gather.12
  337.9 46.1 all-gather.14
  386.7 46.1 all-gather.16
  456.1 59.0 reduce-scatter.21
  517.5 59.9 reduce-scatter.19
  775.1 26.9 reduce-scatter.23
  804.4 26.3 reduce-scatter.25
  836.6 59.9 reduce-scatter.27
  901.2 90.5 reduce-scatter.33
  996.8 89.5 reduce-scatter.35
  1090.8 89.5 reduce-scatter.37
  1185.2 64.7 reduce-scatter.41
  1254.5 57.0 reduce-scatter.29
  1316.1 57.0 reduce-scatter.31
  1378.2 64.2 reduce-scatter.39
